TPU v7x, 128 devices: a whole 4x4x4 slice. The times are simulated.
128 devices in a mesh: layer: 8 (over z, core), energy: 4 (over y), momentum: 4 (over x).
Axes of the slice: x: 4, y: 4, z: 4, core: 2. Of those that a mesh axis runs over, the one named last changes fastest.
Arguments:
- diag_blocks: float32 [4, 16, 4, 2, 384, 384], P('momentum', 'layer', 'energy'), may hold values from -1 to 5
- couplings: float32 [4, 16, 2, 384, 384], P('momentum', 'layer'), may hold values from -0.15625 to 0.15625
- phonon_matrix: float32 [4, 4], replicated, may hold values from -3 to 3
- mode_strength: float32 [3], replicated, may hold values from 0.5 to 2
- transfer_mode: int32 [4], replicated, may hold values from 0 to 2, as said below
- energy_offset: int32 [3], replicated, may hold values from 0 to 1, as said below
Outputs:
- self_energy: float32 [4, 8, 4, 2, 384, 384], P('momentum', 'layer', 'energy')
Inputs may be any that keep to these rules, and one draw needn't show every extreme that they name: `transfer_mode`: every one of the 3 modes is the mode of some transfer. `energy_offset`: some mode has offset 0 and some mode has offset 1.
All inputs are finite; a program needn't handle non-finite values.
Results may differ from a plain program's by a relative error of at most 0.00011.
Values sent between devices are 32-bit elements; how exact they have to be, the bound alone decides.
No kernel may reach another device: no remote copies, remote signals or barrier semaphores. Data moves between devices by JAX's collectives and lax.ppermute only.
A program may use at most 64 MiB of HBM per device.

v0:
```python
import jax
import jax.numpy as jnp
from jax import lax
from jax.experimental import pallas as pl
from jax.experimental.pallas import tpu as pltpu
from jax.sharding import PartitionSpec as P

F32 = jnp.float32
BF16 = jnp.bfloat16


def from_behind(block, axis, distance):
    devices = range(lax.axis_size(axis))
    route = [(i - distance, i) for i in devices if i - distance in devices]
    return lax.ppermute(block, axis, route)


def split(value):
    high = value.astype(BF16)
    return high, (value - high.astype(F32)).astype(BF16)


def put_left(left_high, left_low, rows, real, imag):
    n = real.shape[-1]
    for part, at in ((real, 0), (imag, n)):
        high, low = split(part)
        left_high[rows, at : at + n] = high
        left_low[rows, at : at + n] = low


def put_right(right_high, right_low, real, imag):
    n = real.shape[-1]
    for ref, r, i in zip((right_high, right_low), split(real), split(imag)):
        ref[0:n, 0:n] = r
        ref[0:n, n : 2 * n] = i
        ref[n : 2 * n, 0:n] = -i
        ref[n : 2 * n, n : 2 * n] = r


def product(out, rows, left_high, left_low, right_high, right_low):
    width = right_high.shape[1]
    step = 256
    for at in range(0, width, step):
        columns = slice(at, at + step)
        high = right_high[:, columns]
        low = right_low[:, columns]
        lh = left_high[rows, :]
        out[rows, columns] = (
            jnp.dot(lh, high, preferred_element_type=F32)
            + jnp.dot(lh, low, preferred_element_type=F32)
            + jnp.dot(left_low[rows, :], high, preferred_element_type=F32)
        )


def inverse_diagonal(real, imag):
    n = real.shape[-1]
    rows, columns = [], []
    on = lax.broadcasted_iota(jnp.int32, (128, 128), 0) == lax.broadcasted_iota(
        jnp.int32, (128, 128), 1
    )
    for at in range(0, n, 128):
        s = slice(at, at + 128)
        tiles = [jnp.where(on, part[s, s], 0.0) for part in (real, imag)]
        columns.append([jnp.sum(t, axis=1, keepdims=True) for t in tiles])
        rows.append([jnp.sum(t, axis=0, keepdims=True) for t in tiles])
    result = []
    for pieces, axis in ((rows, 1), (columns, 0)):
        dr = jnp.concatenate([p[0] for p in pieces], axis=axis)
        di = jnp.concatenate([p[1] for p in pieces], axis=axis)
        modulus = dr * dr + di * di
        result += [dr / modulus, -di / modulus]
    return result


def refined_inverse(real, imag, scratch):
    left_high, left_low, right_high, right_low, out = scratch
    n = real.shape[-1]
    rows = slice(0, n)
    row_real, row_imag, col_real, col_imag = inverse_diagonal(real, imag)
    eye = (
        lax.broadcasted_iota(jnp.int32, (n, n), 0) == lax.broadcasted_iota(jnp.int32, (n, n), 1)
    ).astype(F32)
    m_real = real * row_real - imag * row_imag - eye
    m_imag = real * row_imag + imag * row_real
    put_left(left_high, left_low, rows, m_real, m_imag)
    put_right(right_high, right_low, m_real, m_imag)
    product(out, rows, left_high, left_low, right_high, right_low)
    t_real = out[rows, 0:n]
    t_imag = out[rows, n : 2 * n]
    put_right(right_high, right_low, t_real, t_imag)
    q_real = eye - m_real + t_real
    q_imag = t_imag - m_imag
    product(out, rows, left_high, left_low, right_high, right_low)
    q_real = q_real - out[rows, 0:n]
    q_imag = q_imag - out[rows, n : 2 * n]
    return col_real * q_real - col_imag * q_imag, col_real * q_imag + col_imag * q_real


def odd_kernel(odd, coupling, inverse, left_odd, edge, *scratch):
    left_high, left_low, right_high, right_low, out = scratch
    n = odd.shape[-1]
    rows = slice(0, n)
    real, imag = refined_inverse(odd[0], odd[1], scratch)
    inverse[:, 0:n] = real
    inverse[:, n : 2 * n] = imag
    put_right(right_high, right_low, real, imag)
    put_left(left_high, left_low, rows, coupling[0].T, -coupling[1].T)
    product(left_odd, rows, left_high, left_low, right_high, right_low)
    put_left(left_high, left_low, rows, left_odd[:, 0:n], left_odd[:, n : 2 * n])
    put_right(right_high, right_low, coupling[0], coupling[1])
    product(edge, rows, left_high, left_low, right_high, right_low)


def coupling_kernel(inverse, left_odd, even, coupling, before, upper, lower, *scratch):
    left_high, left_low, right_high, right_low, out = scratch
    n = even.shape[-1]
    rows, more = slice(0, n), slice(n, 2 * n)
    put_left(left_high, left_low, rows, coupling[0, 0], coupling[0, 1])
    put_right(right_high, right_low, inverse[:, 0:n], inverse[:, n : 2 * n])
    product(out, rows, left_high, left_low, right_high, right_low)
    put_left(left_high, left_low, rows, out[rows, 0:n], out[rows, n : 2 * n])
    put_left(left_high, left_low, more, left_odd[:, 0:n], left_odd[:, n : 2 * n])
    put_right(right_high, right_low, coupling[1, 0], coupling[1, 1])
    product(out, rows, left_high, left_low, right_high, right_low)
    upper[...] = -out[rows, :]
    put_right(right_high, right_low, coupling[0, 0].T, -coupling[0, 1].T)
    product(out, slice(0, 2 * n), left_high, left_low, right_high, right_low)
    lower[...] = -out[more, :]
    before[:, 0:n] = even[0] - out[rows, 0:n]
    before[:, n : 2 * n] = even[1] - out[rows, n : 2 * n]


def reduced_kernel(before, arrived, reduced, inverse, *scratch):
    n = before.shape[0]
    real = before[:, 0:n] - arrived[:, 0:n]
    imag = before[:, n : 2 * n] - arrived[:, n : 2 * n]
    reduced[:, 0:n] = real
    reduced[:, n : 2 * n] = imag
    real, imag = refined_inverse(real, imag, scratch)
    inverse[:, 0:n] = real
    inverse[:, n : 2 * n] = imag


def term_kernel(first, middle, last, term, *scratch):
    left_high, left_low, right_high, right_low, out = scratch
    n = first.shape[0]
    rows = slice(0, n)
    put_left(left_high, left_low, rows, first[:, 0:n], first[:, n : 2 * n])
    put_right(right_high, right_low, middle[:, 0:n], middle[:, n : 2 * n])
    product(out, rows, left_high, left_low, right_high, right_low)
    put_left(left_high, left_low, rows, out[rows, 0:n], out[rows, n : 2 * n])
    put_right(right_high, right_low, last[:, 0:n], last[:, n : 2 * n])
    product(term, rows, left_high, left_low, right_high, right_low)


def greens_kernel(reduced, upper_term, lower_term, greens, *scratch):
    n = reduced.shape[0]
    real = reduced[:, 0:n] - upper_term[:, 0:n] - lower_term[:, 0:n]
    imag = reduced[:, n : 2 * n] - upper_term[:, n : 2 * n] - lower_term[:, n : 2 * n]
    real, imag = refined_inverse(real, imag, scratch)
    greens[0] = real
    greens[1] = imag


def mix_kernel(phonon, strength, transfer, offset, blocks, mixed):
    energies, momenta, depth, width = blocks.shape
    stay, move = [], []
    for q in range(momenta):
        mode = transfer[q]
        weight = strength[mode]
        still = offset[mode] == 0
        stay.append(jnp.where(still, 2.0 * weight, 0.0))
        move.append(jnp.where(still, 0.0, weight))
    fold = [[phonon[e, f] for f in range(energies)] for e in range(energies)]
    for at in range(0, width, 128):
        columns = slice(at, at + 128)

        def rows_of(i, carry):
            rows = pl.ds(pl.multiple_of(i * 8, 8), 8)
            folded = []
            for k in range(momenta):
                g = [blocks[f, k, rows, columns] for f in range(energies)]
                folded.append(
                    [sum(fold[e][f] * g[f] for f in range(energies)) for e in range(energies)]
                )
            for k in range(momenta):
                moved = [
                    sum(move[q] * folded[(k - q) % momenta][e] for q in range(momenta))
                    for e in range(energies)
                ]
                for e in range(energies):
                    total = sum(stay[q] * folded[(k - q) % momenta][e] for q in range(momenta))
                    if e > 0:
                        total = total + moved[e - 1]
                    if e + 1 < energies:
                        total = total + moved[e + 1]
                    mixed[e, k, rows, columns] = total
            return carry

        lax.fori_loop(0, depth // 8, rows_of, 0)


def call(kernel, outs, operands, specs=None, products=0, tall=1, wide=True):
    n = operands[0].shape[-2]
    whole = pl.BlockSpec(memory_space=pltpu.VMEM)
    scratch = [
        pltpu.VMEM((tall * n, 2 * n), BF16),
        pltpu.VMEM((tall * n, 2 * n), BF16),
        pltpu.VMEM((2 * n, 2 * n), BF16),
        pltpu.VMEM((2 * n, 2 * n), BF16),
        pltpu.VMEM((tall * n, 2 * n), F32),
    ]
    return pl.pallas_call(
        kernel,
        out_shape=[jax.ShapeDtypeStruct(s, F32) for s in outs],
        grid=(1,),
        in_specs=specs or [pl.BlockSpec(o.shape, lambda i, r=o.ndim: (0,) * r) for o in operands],
        out_specs=[pl.BlockSpec(s, lambda i, r=len(s): (0,) * r) for s in outs],
        scratch_shapes=scratch,
        compiler_params=pltpu.CompilerParams(vmem_limit_bytes=40 * 1024 * 1024),
        cost_estimate=pl.CostEstimate(
            flops=products * 24 * n**3,
            bytes_accessed=8 * n * n * (len(outs) + len(operands)),
            transcendentals=0,
        ),
    )(*operands)


def body(diag_blocks, couplings, phonon_matrix, mode_strength, transfer_mode, energy_offset):
    n = diag_blocks.shape[-1]
    wide = (n, 2 * n)

    def diag(which):
        return pl.BlockSpec((None, None, None, 2, n, n), lambda i: (0, which, 0, 0, 0, 0))

    def whole(shape):
        return pl.BlockSpec(shape, lambda i: (0,) * len(shape))

    odd_coupling = pl.BlockSpec((None, None, 2, n, n), lambda i: (0, 1, 0, 0, 0))
    both = pl.BlockSpec((None, 2, 2, n, n), lambda i: (0, 0, 0, 0, 0))
    inverse, left_odd, edge = call(
        odd_kernel, [wide] * 3, (diag_blocks, couplings), [diag(1), odd_coupling], 4
    )
    arrived = from_behind(edge, "layer", 1)
    before, upper, lower = call(
        coupling_kernel,
        [wide] * 3,
        (inverse, left_odd, diag_blocks, couplings),
        [whole(wide), whole(wide), diag(0), both],
        4,
        tall=2,
    )
    reduced, reduced_inverse = call(reduced_kernel, [wide] * 2, (before, arrived), products=2)
    neighbour = from_behind(reduced_inverse, "layer", -1)
    (lower_term,) = call(term_kernel, [wide], (lower, reduced_inverse, upper), products=2)
    from_below = from_behind(lower_term, "layer", 1)
    (upper_term,) = call(term_kernel, [wide], (upper, neighbour, lower), products=2)
    (greens,) = call(greens_kernel, [(2, n, n)], (reduced, upper_term, from_below), products=2)
    energies, momenta = lax.axis_size("energy"), lax.axis_size("momentum")
    group = energies * momenta
    depth = 2 * n // group
    axes = ("energy", "momentum")
    spread = lax.all_to_all(
        greens.reshape(group, depth, n), axes, split_axis=0, concat_axis=0, tiled=True
    )
    block = (energies, momenta, depth, n)
    small = pl.BlockSpec(memory_space=pltpu.SMEM)
    mixed = pl.pallas_call(
        mix_kernel,
        out_shape=jax.ShapeDtypeStruct(block, F32),
        grid=(1,),
        in_specs=[small] * 4 + [whole(block)],
        out_specs=whole(block),
    )(phonon_matrix, mode_strength, transfer_mode, energy_offset, spread.reshape(block))
    returned = lax.all_to_all(
        mixed.reshape(group, depth, n), axes, split_axis=0, concat_axis=0, tiled=True
    )
    return returned.reshape(1, 1, 1, 2, n, n)


def solution(mesh):
    return jax.shard_map(
        body,
        mesh=mesh,
        in_specs=(
            P("momentum", "layer", "energy", None, None, None),
            P("momentum", "layer", None, None, None),
            P(),
            P(),
            P(),
            P(),
        ),
        out_specs=P("momentum", "layer", "energy", None, None, None),
        check_vma=False,
    )
```

profile of v0, /device:TPU:32, one launch (start us, length us, event | category | flops | bytes accessed | tf_op | source)
XLA Modules:
  0.0 112.4 jit_solution(6195092122623486748)
XLA Ops:
  0.0 0.0 copy-start
  0.0 1.7 %copy-done = f32[1,2,1,2,384,384]{5,4,3,2,1,0:T(8,128)S(1)} copy-done((f32[1,2,1,2,384,384]{5,4,3,2,1,0:T(8,128)S(1)}, f32[1,2,1,2,384,384]{5,4,3,2,1,0:T(8,128)}, u32[]{:S(2)}) %copy-start) | copy-done | bytes 2359320
  1.7 0.0 copy-start.1
  1.7 1.7 %copy-done.1 = f32[1,2,2,384,384]{4,3,2,1,0:T(8,128)S(1)} copy-done((f32[1,2,2,384,384]{4,3,2,1,0:T(8,128)S(1)}, f32[1,2,2,384,384]{4,3,2,1,0:T(8,128)}, u32[]{:S(2)}) %copy-start.1) | copy-done | bytes 2359320
  3.3 8.5 %shard_map.64 = (f32[384,768]{1,0:T(8,128)S(1)}, f32[384,768]{1,0:T(8,128)S(1)}, f32[384,768]{1,0:T(8,128)S(1)}) custom-call(f32[1,2,1,2,384,384]{5,4,3,2,1,0:T(8,128)S(1)} %copy-done, f32[1,2,2,384,384]{4,3,2,1,0:T(8,128)S(1)} %copy-done.1), custom_call_target="tpu_custom_call" | custom-call | flops 5435817984 | bytes 5898240 | tf_op jit(solution)/shard_map/pallas_call | solution.py:213
  11.8 2.1 %collective-permute-start = (f32[384,768]{1,0:T(8,128)S(1)}, f32[384,768]{1,0:T(8,128)S(1)}, u32[]{:S(2)}, u32[]{:S(2)}) collective-permute-start(f32[384,768]{1,0:T(8,128)S(1)} %get-tuple-element.16), channel_id=1, source_target_pairs={{0,16},{16,32},{32,48},{48,64},{64,80},{80,96},{96,112},{1,17},{17... | collective-permute-start | bytes 3538952 | tf_op jit(solution)/shard_map/ppermute | solution.py:15
  13.9 6.7 %shard_map.65 = (f32[384,768]{1,0:T(8,128)S(1)}, f32[384,768]{1,0:T(8,128)S(1)}, f32[384,768]{1,0:T(8,128)S(1)}) custom-call(f32[384,768]{1,0:T(8,128)S(1)} %get-tuple-element.13.inverse, f32[384,768]{1,0:T(8,128)S(1)} %get-tuple-element.14.left_odd, f32[1,2,1,2,384,384]{5,4,3,2,1,0:T(8,128)S(1)} %copy-done, f32[1,2,2,384,384]{4,3,2,1,0:T(8,128)S(1)} %copy-done.1), custom_call_target="tpu_custom_call" | custom-call | flops 5435817984 | bytes 8257536 | tf_op jit(solution)/shard_map/pallas_call | solution.py:213
  20.7 8.7 %collective-permute-done.arrived = f32[384,768]{1,0:T(8,128)S(1)} collective-permute-done((f32[384,768]{1,0:T(8,128)S(1)}, f32[384,768]{1,0:T(8,128)S(1)}, u32[]{:S(2)}, u32[]{:S(2)}) %collective-permute-start) | collective-permute-done | bytes 1179680 | tf_op jit(solution)/shard_map/ppermute | solution.py:15
  29.3 4.3 %shard_map.66 = (f32[384,768]{1,0:T(8,128)S(1)}, f32[384,768]{1,0:T(8,128)S(1)}) custom-call(f32[384,768]{1,0:T(8,128)S(1)} %get-tuple-element.15.before, f32[384,768]{1,0:T(8,128)S(1)} %collective-permute-done.arrived), custom_call_target="tpu_custom_call" | custom-call | flops 2717908992 | bytes 4718592 | tf_op jit(solution)/shard_map/pallas_call | solution.py:213
  33.7 1.9 %collective-permute-start.1 = (f32[384,768]{1,0:T(8,128)S(1)}, f32[384,768]{1,0:T(8,128)S(1)}, u32[]{:S(2)}, u32[]{:S(2)}) collective-permute-start(f32[384,768]{1,0:T(8,128)S(1)} %get-tuple-element.19.middle), channel_id=1, source_target_pairs={{16,0},{32,16},{48,32},{64,48},{80,64},{96,80},{112,96},{17,1},{33... | collective-permute-start | bytes 3538952 | tf_op jit(solution)/shard_map/ppermute | solution.py:15
  35.6 4.2 %shard_map.68 = f32[384,768]{1,0:T(8,128)S(1)} custom-call(f32[384,768]{1,0:T(8,128)S(1)} %get-tuple-element.20.last.first, f32[384,768]{1,0:T(8,128)S(1)} %get-tuple-element.19.middle, f32[384,768]{1,0:T(8,128)S(1)} %get-tuple-element.18.first.last), custom_call_target="tpu_custom_call" | custom-call | flops 2717908992 | bytes 4718592 | tf_op jit(solution)/shard_map/pallas_call | solution.py:213
  39.8 2.6 %collective-permute-start.2 = (f32[384,768]{1,0:T(8,128)S(1)}, f32[384,768]{1,0:T(8,128)S(1)}, u32[]{:S(2)}, u32[]{:S(2)}) collective-permute-start(f32[384,768]{1,0:T(8,128)S(1)} %shard_map.68), channel_id=1, source_target_pairs={{0,16},{16,32},{32,48},{48,64},{64,80},{80,96},{96,112},{1,17},{17... | collective-permute-start | bytes 3538952 | tf_op jit(solution)/shard_map/ppermute | solution.py:15
  42.5 6.9 %collective-permute-done.1.middle = f32[384,768]{1,0:T(8,128)S(1)} collective-permute-done((f32[384,768]{1,0:T(8,128)S(1)}, f32[384,768]{1,0:T(8,128)S(1)}, u32[]{:S(2)}, u32[]{:S(2)}) %collective-permute-start.1) | collective-permute-done | bytes 1179680 | tf_op jit(solution)/shard_map/ppermute | solution.py:15
  49.3 4.2 %shard_map.67.upper_term = f32[384,768]{1,0:T(8,128)S(1)} custom-call(f32[384,768]{1,0:T(8,128)S(1)} %get-tuple-element.18.first.last, f32[384,768]{1,0:T(8,128)S(1)} %collective-permute-done.1.middle, f32[384,768]{1,0:T(8,128)S(1)} %get-tuple-element.20.last.first), custom_call_target="tpu_custom_call" | custom-call | flops 2717908992 | bytes 4718592 | tf_op jit(solution)/shard_map/pallas_call | solution.py:213
  53.5 3.8 %collective-permute-done.2.lower_term = f32[384,768]{1,0:T(8,128)S(1)} collective-permute-done((f32[384,768]{1,0:T(8,128)S(1)}, f32[384,768]{1,0:T(8,128)S(1)}, u32[]{:S(2)}, u32[]{:S(2)}) %collective-permute-start.2) | collective-permute-done | bytes 1179680 | tf_op jit(solution)/shard_map/ppermute | solution.py:15
  57.3 4.4 %shard_map.69 = f32[2,384,384]{2,1,0:T(8,128)S(1)} custom-call(f32[384,768]{1,0:T(8,128)S(1)} %get-tuple-element.17.reduced, f32[384,768]{1,0:T(8,128)S(1)} %shard_map.67.upper_term, f32[384,768]{1,0:T(8,128)S(1)} %collective-permute-done.2.lower_term), custom_call_target="tpu_custom_call" | custom-call | flops 2717908992 | bytes 4718592 | tf_op jit(solution)/shard_map/pallas_call | solution.py:213
  61.7 25.2 %all_to_all.10 = f32[16,48,384]{2,1,0:T(8,128)} all-to-all(f32[16,48,384]{2,1,0:T(8,128)S(1)} %bitcast.4), channel_id=1, replica_groups=mesh['layer'=8,'energy'=4,'momentum'=4] {'energy','momentum'}, dimensions={0} | all-to-all | bytes 2359296 | tf_op jit(solution)/shard_map/all_to_all | solution.py:263
  87.0 3.3 %shard_map.70 = f32[4,4,48,384]{3,2,1,0:T(8,128)} custom-call(f32[4,4]{1,0:T(4,128)} %phonon.1, f32[3]{0:T(128)} %strength.1, s32[4]{0:T(128)} %transfer.1, s32[3]{0:T(128)} %offset.1, f32[4,4,48,384]{3,2,1,0:T(8,128)} %bitcast.6), custom_call_target="tpu_custom_call" | custom-call | tf_op jit(solution)/shard_map/pallas_call | solution.py:268
  90.3 21.1 %all_to_all.11 = f32[16,48,384]{2,1,0:T(8,128)S(1)} all-to-all(f32[16,48,384]{2,1,0:T(8,128)} %bitcast.7), channel_id=1, replica_groups=mesh['layer'=8,'energy'=4,'momentum'=4] {'energy','momentum'}, dimensions={0} | all-to-all | bytes 2359296 | tf_op jit(solution)/shard_map/all_to_all | solution.py:275
  111.4 1.0 copy.8
Async XLA Ops:
  0.0 1.7 %copy-start = (f32[1,2,1,2,384,384]{5,4,3,2,1,0:T(8,128)S(1)}, f32[1,2,1,2,384,384]{5,4,3,2,1,0:T(8,128)}, u32[]{:S(2)}) copy-start(f32[1,2,1,2,384,384]{5,4,3,2,1,0:T(8,128)} %even.1) | copy-start | bytes 7077892
  1.7 1.7 %copy-start.1 = (f32[1,2,2,384,384]{4,3,2,1,0:T(8,128)S(1)}, f32[1,2,2,384,384]{4,3,2,1,0:T(8,128)}, u32[]{:S(2)}) copy-start(f32[1,2,2,384,384]{4,3,2,1,0:T(8,128)} %coupling.3) | copy-start | bytes 7077892
  11.8 17.5 %collective-permute-start = (f32[384,768]{1,0:T(8,128)S(1)}, f32[384,768]{1,0:T(8,128)S(1)}, u32[]{:S(2)}, u32[]{:S(2)}) collective-permute-start(f32[384,768]{1,0:T(8,128)S(1)} %get-tuple-element.16), channel_id=1, source_target_pairs={{0,16},{16,32},{32,48},{48,64},{64,80},{80,96},{96,112},{1,17},{17... | collective-permute-start | bytes 3538952 | tf_op jit(solution)/shard_map/ppermute | solution.py:15
  33.7 15.6 %collective-permute-start.1 = (f32[384,768]{1,0:T(8,128)S(1)}, f32[384,768]{1,0:T(8,128)S(1)}, u32[]{:S(2)}, u32[]{:S(2)}) collective-permute-start(f32[384,768]{1,0:T(8,128)S(1)} %get-tuple-element.19.middle), channel_id=1, source_target_pairs={{16,0},{32,16},{48,32},{64,48},{80,64},{96,80},{112,96},{17,1},{33... | collective-permute-start | bytes 3538952 | tf_op jit(solution)/shard_map/ppermute | solution.py:15
  39.8 17.5 %collective-permute-start.2 = (f32[384,768]{1,0:T(8,128)S(1)}, f32[384,768]{1,0:T(8,128)S(1)}, u32[]{:S(2)}, u32[]{:S(2)}) collective-permute-start(f32[384,768]{1,0:T(8,128)S(1)} %shard_map.68), channel_id=1, source_target_pairs={{0,16},{16,32},{32,48},{48,64},{64,80},{80,96},{96,112},{1,17},{17... | collective-permute-start | bytes 3538952 | tf_op jit(solution)/shard_map/ppermute | solution.py:15
where the time goes:
time: 113 us; the launch traced here: 112 us
  blocking collectives  46.3 us (41%)
  Pallas kernels  35.6 us (32%)
  waiting for transfers between devices  19.4 us (17%)
  starting transfers between devices  6.65 us (6%)
  local copies, waits for them, and re-layouts  4.34 us (4%)
    pallas_call x6, Pallas kernels, call(): pl.pallas_call(kernel, out_shape=[jax.ShapeDtypeStruct(s, F32) for s in o...  32.3 us
    all_to_all x1, blocking collectives, body(): lax.all_to_all(greens.reshape(group, depth, n), axes, split_axis=0, conca...  25.2 us
    all_to_all x1, blocking collectives, body(): lax.all_to_all(mixed.reshape(group, depth, n), axes, split_axis=0, concat...  21.1 us
    ppermute x3, waiting for transfers between devices, from_behind(): return lax.ppermute(block, axis, route)  19.4 us
    ppermute x3, starting transfers between devices, from_behind(): return lax.ppermute(block, axis, route)  6.65 us
    unnamed x5, local copies, waits for them, and re-layouts  4.34 us
    pallas_call x1, Pallas kernels, body(): pl.pallas_call(mix_kernel, out_shape=jax.ShapeDtypeStruct(block, F32), gr...  3.3 us
  transfers between devices with their start and end apart: 3, of which 3 were waited for; matrix products, arithmetic and copies ran while one was open for 0% of the time, Pallas kernels for 13%

commit v1 on v0

v1 whole, which is shorter than its diff:
```python
import jax
import jax.numpy as jnp
from jax import lax
from jax.experimental import pallas as pl
from jax.experimental.pallas import tpu as pltpu
from jax.sharding import PartitionSpec as P

F32 = jnp.float32
BF16 = jnp.bfloat16


def split(value):
    high = value.astype(BF16)
    return high, (value - high.astype(F32)).astype(BF16)


def put_left(left, rows, real, imag):
    n = real.shape[-1]
    for part, at in ((real, 0), (imag, n)):
        for ref, value in zip(left, split(part)):
            ref[rows, at : at + n] = value


def put_right(right, real, imag):
    n = real.shape[-1]
    for ref, r, i in zip(right, split(real), split(imag)):
        ref[0:n, 0:n] = r
        ref[0:n, n : 2 * n] = i
        ref[n : 2 * n, 0:n] = -i
        ref[n : 2 * n, n : 2 * n] = r


def product(out, left, right):
    step = 256
    for at in range(0, right[0].shape[1], step):
        columns = slice(at, at + step)
        high = right[0][:, columns]
        low = right[1][:, columns]
        lh = left[0][...]
        out[:, columns] = (
            jnp.dot(lh, high, preferred_element_type=F32)
            + jnp.dot(lh, low, preferred_element_type=F32)
            + jnp.dot(left[1][...], high, preferred_element_type=F32)
        )


def halves(ref):
    n = ref.shape[0]
    return ref[:, 0:n], ref[:, n : 2 * n]


def inverse_diagonal(real, imag):
    n = real.shape[-1]
    rows, columns = [], []
    on = lax.broadcasted_iota(jnp.int32, (128, 128), 0) == lax.broadcasted_iota(
        jnp.int32, (128, 128), 1
    )
    for at in range(0, n, 128):
        s = slice(at, at + 128)
        tiles = [jnp.where(on, part[s, s], 0.0) for part in (real, imag)]
        columns.append([jnp.sum(t, axis=1, keepdims=True) for t in tiles])
        rows.append([jnp.sum(t, axis=0, keepdims=True) for t in tiles])
    result = []
    for pieces, axis in ((rows, 1), (columns, 0)):
        dr = jnp.concatenate([p[0] for p in pieces], axis=axis)
        di = jnp.concatenate([p[1] for p in pieces], axis=axis)
        modulus = dr * dr + di * di
        result += [dr / modulus, -di / modulus]
    return result


def refined_inverse(real, imag, left, first, second, out):
    n = real.shape[-1]
    rows = slice(0, n)
    row_real, row_imag, col_real, col_imag = inverse_diagonal(real, imag)
    eye = (
        lax.broadcasted_iota(jnp.int32, (n, n), 0) == lax.broadcasted_iota(jnp.int32, (n, n), 1)
    ).astype(F32)
    m_real = real * row_real - imag * row_imag - eye
    m_imag = real * row_imag + imag * row_real
    put_left(left, rows, m_real, m_imag)
    put_right(first, m_real, m_imag)
    product(out, left, first)
    t_real, t_imag = halves(out)
    put_right(second, t_real, t_imag)
    q_real = eye - m_real + t_real
    q_imag = t_imag - m_imag
    product(out, left, second)
    s_real, s_imag = halves(out)
    q_real = q_real - s_real
    q_imag = q_imag - s_imag
    return col_real * q_real - col_imag * q_imag, col_real * q_imag + col_imag * q_real


def parity():
    return lax.axis_index("layer") % 2


def sandwich(which, coupling, even, inverse, left, result, scratch):
    lefts, others, first, second = scratch
    n = even.shape[-1]
    rows = slice(0, n)
    is_even = which == 0
    real, imag = coupling[0], coupling[1]
    real_t, imag_t = real.T, -imag.T
    put_left(lefts, rows, jnp.where(is_even, real, real_t), jnp.where(is_even, imag, imag_t))
    put_right(second, jnp.where(is_even, real_t, real), jnp.where(is_even, imag_t, imag))
    put_right(first, *inverse)
    product(left, lefts, first)
    put_left(others, rows, *halves(left))
    product(result, others, second)
    for part in range(2):
        columns = slice(part * n, (part + 1) * n)
        term = result[:, columns]
        result[:, columns] = jnp.where(is_even, even[part] - term, term)


def first_kernel(diag, couplings, inverse, left, result, odd, even, coupling, sems, *scratch):
    n = odd.shape[-1]
    which = parity()
    copies = [
        pltpu.make_async_copy(diag.at[0, 1, 0, 0], odd.at[0], sems.at[0]),
        pltpu.make_async_copy(diag.at[0, 1, 0, 1], odd.at[1], sems.at[1]),
        pltpu.make_async_copy(couplings.at[0, which], coupling, sems.at[2]),
        pltpu.make_async_copy(diag.at[0, 0, 0], even, sems.at[3]),
    ]
    for copy in copies:
        copy.start()
    copies[0].wait()
    copies[1].wait()
    pairs = [(scratch[i], scratch[i + 1]) for i in range(0, 8, 2)]
    lefts, others, first, second = pairs
    value = refined_inverse(odd[0], odd[1], lefts, first, second, result)
    inverse[:, 0:n] = value[0]
    inverse[:, n : 2 * n] = value[1]
    copies[2].wait()
    copies[3].wait()
    sandwich(which, coupling, even, value, left, result, pairs)


def second_kernel(diag, couplings, inverse, left, result, even, coupling, sems, *scratch):
    which = 1 - parity()
    copies = [
        pltpu.make_async_copy(couplings.at[0, which], coupling, sems.at[0]),
        pltpu.make_async_copy(diag.at[0, 0, 0], even, sems.at[1]),
    ]
    for copy in copies:
        copy.start()
    for copy in copies:
        copy.wait()
    pairs = [(scratch[i], scratch[i + 1]) for i in range(0, 8, 2)]
    sandwich(which, coupling, even, halves(inverse), left, result, pairs)


def cross_kernel(couplings, slow, fast, one, two, coupling, sems, *scratch):
    n = slow.shape[0]
    rows = slice(0, n)
    is_even = parity() == 0
    copy = pltpu.make_async_copy(couplings.at[0], coupling, sems.at[0])
    copy.start()
    lefts, others, first, second = [(scratch[i], scratch[i + 1]) for i in range(0, 8, 2)]
    put_left(lefts, rows, *[-v for v in halves(slow)])
    put_left(others, rows, *[-v for v in halves(fast)])
    copy.wait()
    even_right = (coupling[0, 0].T, -coupling[0, 1].T)
    odd_right = (coupling[1, 0], coupling[1, 1])
    put_right(first, *[jnp.where(is_even, o, e) for e, o in zip(even_right, odd_right)])
    put_right(second, *[jnp.where(is_even, e, o) for e, o in zip(even_right, odd_right)])
    product(one, lefts, first)
    product(two, others, second)


def reduced_term(start, real, imag, before, after, reduced, term, scratch):
    lefts, others, first, second = scratch
    n = real.shape[-1]
    rows = slice(0, n)
    value = refined_inverse(real, imag, lefts, first, second, term)
    put_left(others, rows, *halves(before))
    put_right(first, *value)
    product(term, others, first)
    put_left(lefts, rows, *halves(term))
    put_right(second, *halves(after))
    product(term, lefts, second)


def chip_kernel(mine, other, one, two, reduced, term, *scratch):
    n = mine.shape[0]
    is_even = parity() == 0
    parts = []
    for part, (a, b) in enumerate(zip(halves(mine), halves(other))):
        value = jnp.where(is_even, b - a, a - b)
        reduced[:, part * n : (part + 1) * n] = value
        parts.append(value)
    pairs = [(scratch[i], scratch[i + 1]) for i in range(0, 8, 2)]
    reduced_term(is_even, *parts, one, two, reduced, term, pairs)


def border_kernel(mine, other, one, two, reduced, chip_term, partial, term, *scratch):
    n = mine.shape[0]
    index = lax.axis_index("layer")
    is_even = index % 2 == 0
    is_last = index == lax.axis_size("layer") - 1
    parts = []
    for a, b in zip(halves(mine), halves(other)):
        parts.append(jnp.where(is_even, a - b, b - a))
    pairs = [(scratch[i], scratch[i + 1]) for i in range(0, 8, 2)]
    reduced_term(is_even, *parts, two, one, reduced, term, pairs)
    for part in range(2):
        columns = slice(part * n, (part + 1) * n)
        value = jnp.where(is_last, 0.0, term[:, columns])
        term[:, columns] = value
        partial[:, columns] = jnp.where(is_even, parts[part], reduced[:, columns]) - jnp.where(
            is_even, chip_term[:, columns], value
        )


def subtract_kernel(partial, border_term, rest, *scratch):
    rest[...] = partial[...] - border_term[...]


def greens_kernel(rest, chip_term, greens, *scratch):
    lefts, others, first, second = [(scratch[i], scratch[i + 1]) for i in range(0, 8, 2)]
    real, imag = [a - b for a, b in zip(halves(rest), halves(chip_term))]
    real, imag = refined_inverse(real, imag, lefts, first, second, scratch[8])
    greens[0] = real
    greens[1] = imag


def mix_kernel(phonon, strength, transfer, offset, blocks, mixed):
    energies, momenta, depth, width = blocks.shape
    stay, move = [], []
    for q in range(momenta):
        mode = transfer[q]
        weight = strength[mode]
        still = offset[mode] == 0
        stay.append(jnp.where(still, 2.0 * weight, 0.0))
        move.append(jnp.where(still, 0.0, weight))
    fold = [[phonon[e, f] for f in range(energies)] for e in range(energies)]
    for at in range(0, width, 128):
        columns = slice(at, at + 128)

        def rows_of(i, carry):
            rows = pl.ds(pl.multiple_of(i * 8, 8), 8)
            folded = []
            for k in range(momenta):
                g = [blocks[f, k, rows, columns] for f in range(energies)]
                folded.append(
                    [sum(fold[e][f] * g[f] for f in range(energies)) for e in range(energies)]
                )
            for k in range(momenta):
                moved = [
                    sum(move[q] * folded[(k - q) % momenta][e] for q in range(momenta))
                    for e in range(energies)
                ]
                for e in range(energies):
                    total = sum(stay[q] * folded[(k - q) % momenta][e] for q in range(momenta))
                    if e > 0:
                        total = total + moved[e - 1]
                    if e + 1 < energies:
                        total = total + moved[e + 1]
                    mixed[e, k, rows, columns] = total
            return carry

        lax.fori_loop(0, depth // 8, rows_of, 0)


def call(kernel, outs, operands, products, extra=(), sems=0):
    n = operands[0].shape[-2]

    def spec(shape):
        if len(shape) > 2 and shape[-1] == shape[-2]:
            return pl.BlockSpec(memory_space=pl.ANY)
        return pl.BlockSpec(shape, lambda i: (0,) * len(shape))

    scratch = [pltpu.VMEM(s, F32) for s in extra]
    if sems:
        scratch.append(pltpu.SemaphoreType.DMA((sems,)))
    scratch += [pltpu.VMEM((n, 2 * n), BF16)] * 4 + [pltpu.VMEM((2 * n, 2 * n), BF16)] * 4
    if kernel is subtract_kernel:
        scratch = []
    if kernel is greens_kernel:
        scratch.append(pltpu.VMEM((n, 2 * n), F32))
    return pl.pallas_call(
        kernel,
        out_shape=[jax.ShapeDtypeStruct(s, F32) for s in outs],
        grid=(1,),
        in_specs=[spec(o.shape) for o in operands],
        out_specs=[pl.BlockSpec(s, lambda i, r=len(s): (0,) * r) for s in outs],
        scratch_shapes=scratch,
        compiler_params=pltpu.CompilerParams(vmem_limit_bytes=28 * 1024 * 1024),
        cost_estimate=pl.CostEstimate(
            flops=3 * 10**10,
            bytes_accessed=1,
            transcendentals=0,
        ),
    )(*operands)


def swap(block, axis, first):
    route = []
    for i in range(first, lax.axis_size(axis) - 1, 2):
        route += [(i, i + 1), (i + 1, i)]
    return lax.ppermute(block, axis, route)


def ahead(block, axis, first):
    return lax.ppermute(
        block, axis, [(i, i + 1) for i in range(first, lax.axis_size(axis) - 1, 2)]
    )


def body(diag_blocks, couplings, phonon_matrix, mode_strength, transfer_mode, energy_offset):
    n = diag_blocks.shape[-1]
    wide, square = (n, 2 * n), (2, n, n)

    def whole(shape):
        return pl.BlockSpec(shape, lambda i: (0,) * len(shape))

    diag_blocks, couplings = [
        pltpu.with_memory_space_constraint(v, pltpu.HBM) for v in (diag_blocks, couplings)
    ]
    inverse, slow, border = call(
        first_kernel, [wide] * 3, (diag_blocks, couplings), 4, [square] * 3, 4
    )
    border_other = swap(border, "layer", 1)
    fast, chip = call(
        second_kernel, [wide] * 2, (diag_blocks, couplings, inverse), 2, [square] * 2, 2
    )
    chip_other = swap(chip, "layer", 0)
    one, two = call(cross_kernel, [wide] * 2, (couplings, slow, fast), 2, [(2,) + square], 1)
    reduced, chip_term = call(chip_kernel, [wide] * 2, (chip, chip_other, one, two), 4)
    from_border = ahead(chip_term, "layer", 1)
    partial, border_term = call(
        border_kernel, [wide] * 2, (border, border_other, one, two, reduced, chip_term), 4
    )
    from_chip = ahead(border_term, "layer", 0)
    (rest,) = call(subtract_kernel, [wide], (partial, from_border), 0)
    (greens,) = call(greens_kernel, [square], (rest, from_chip), 2)
    energies, momenta = lax.axis_size("energy"), lax.axis_size("momentum")
    group = energies * momenta
    depth = 2 * n // group
    axes = ("energy", "momentum")
    spread = lax.all_to_all(
        greens.reshape(group, depth, n), axes, split_axis=0, concat_axis=0, tiled=True
    )
    block = (energies, momenta, depth, n)
    small = pl.BlockSpec(memory_space=pltpu.SMEM)
    mixed = pl.pallas_call(
        mix_kernel,
        out_shape=jax.ShapeDtypeStruct(block, F32),
        grid=(1,),
        in_specs=[small] * 4 + [whole(block)],
        out_specs=whole(block),
        compiler_params=pltpu.CompilerParams(vmem_limit_bytes=12 * 1024 * 1024),
    )(phonon_matrix, mode_strength, transfer_mode, energy_offset, spread.reshape(block))
    returned = lax.all_to_all(
        mixed.reshape(group, depth, n), axes, split_axis=0, concat_axis=0, tiled=True
    )
    return returned.reshape(1, 1, 1, 2, n, n)


def solution(mesh):
    return jax.shard_map(
        body,
        mesh=mesh,
        in_specs=(
            P("momentum", "layer", "energy", None, None, None),
            P("momentum", "layer", None, None, None),
            P(),
            P(),
            P(),
            P(),
        ),
        out_specs=P("momentum", "layer", "energy", None, None, None),
        check_vma=False,
    )
```

time: 113 us -> 106 us (0.938)
  the two profiles are of different devices: /device:TPU:32 before, /device:TPU:0 now
where the time goes in v1:
time: 106 us; the launch traced here: 105 us
  blocking collectives  47.3 us (45%)
  Pallas kernels  44 us (42%)
  starting transfers between devices  10.5 us (10%)
  waiting for transfers between devices  2.25 us (2%)
    pallas_call x7, Pallas kernels, call(): pl.pallas_call(kernel, out_shape=[jax.ShapeDtypeStruct(s, F32) for s in o...  42.4 us
    all_to_all x1, blocking collectives, body(): lax.all_to_all(greens.reshape(group, depth, n), axes, split_axis=0, conca...  26.1 us
    all_to_all x1, blocking collectives, body(): lax.all_to_all(mixed.reshape(group, depth, n), axes, split_axis=0, concat...  21.2 us
    ppermute x2, starting transfers between devices, ahead(): lax.ppermute(block, axis, [(i, i + 1) for i in range(first, lax.axis_size...  6.21 us
    ppermute x2, starting transfers between devices, swap(): return lax.ppermute(block, axis, route)  4.28 us
    ppermute x2, waiting for transfers between devices, ahead(): lax.ppermute(block, axis, [(i, i + 1) for i in range(first, lax.axis_size...  2.24 us
  transfers between devices with their start and end apart: 4, of which 1 were waited for; matrix products, arithmetic and copies ran while one was open for 0% of the time, Pallas kernels for 27%

profile of v1, /device:TPU:0, one launch (start us, length us, event | category | flops | bytes accessed | tf_op | source)
XLA Modules:
  0.0 105.3 jit_solution(6588650165161616046)
XLA Ops:
  0.0 9.9 %shard_map.64 = (f32[384,768]{1,0:T(8,128)S(1)}, f32[384,768]{1,0:T(8,128)S(1)}, f32[384,768]{1,0:T(8,128)S(1)}) custom-call(f32[1,2,1,2,384,384]{5,4,3,2,1,0:T(8,128)} %diag.3, f32[1,2,2,384,384]{4,3,2,1,0:T(8,128)} %couplings.5), custom_call_target="tpu_custom_call" | custom-call | flops 30000001024 | bytes 1 | tf_op jit(solution)/shard_map/pallas_call | solution.py:283
  9.9 0.7 collective-permute-start
  10.7 6.0 %shard_map.65 = (f32[384,768]{1,0:T(8,128)S(1)}, f32[384,768]{1,0:T(8,128)S(1)}) custom-call(f32[1,2,1,2,384,384]{5,4,3,2,1,0:T(8,128)} %diag.3, f32[1,2,2,384,384]{4,3,2,1,0:T(8,128)} %couplings.5, f32[384,768]{1,0:T(8,128)S(1)} %get-tuple-element.18.inverse), custom_call_target="tpu_custom_call" | custom-call | flops 30000001024 | bytes 1 | tf_op jit(solution)/shard_map/pallas_call | solution.py:283
  16.7 3.5 %collective-permute-start.1 = (f32[384,768]{1,0:T(8,128)S(1)}, f32[384,768]{1,0:T(8,128)S(1)}, u32[]{:S(2)}, u32[]{:S(2)}) collective-permute-start(f32[384,768]{1,0:T(8,128)S(1)} %get-tuple-element.22.mine), channel_id=1, source_target_pairs={{0,16},{16,0},{32,48},{48,32},{64,80},{80,64},{96,112},{112,96},{1... | collective-permute-start | bytes 3538952 | tf_op jit(solution)/shard_map/ppermute | solution.py:303
  20.2 5.1 %shard_map.66 = (f32[384,768]{1,0:T(8,128)S(1)}, f32[384,768]{1,0:T(8,128)S(1)}) custom-call(f32[1,2,2,384,384]{4,3,2,1,0:T(8,128)} %couplings.5, f32[384,768]{1,0:T(8,128)S(1)} %get-tuple-element.17.slow, f32[384,768]{1,0:T(8,128)S(1)} %get-tuple-element.19.fast), custom_call_target="tpu_custom_call" | custom-call | flops 30000001024 | bytes 1 | tf_op jit(solution)/shard_map/pallas_call | solution.py:283
  25.3 0.0 collective-permute-done.1.other
  25.3 8.5 %shard_map.67 = (f32[384,768]{1,0:T(8,128)S(1)}, f32[384,768]{1,0:T(8,128)S(1)}) custom-call(f32[384,768]{1,0:T(8,128)S(1)} %get-tuple-element.22.mine, f32[384,768]{1,0:T(8,128)S(1)} %collective-permute-done.1.other, f32[384,768]{1,0:T(8,128)S(1)} %get-tuple-element.20.one, f32[384,768]{1,0:T(8,128)S(1)} %get-tuple-element.21.two), custom_call_target="tpu_custom_call" | custom-call | flops 30000001024 | bytes 1 | tf_op jit(solution)/shard_map/pallas_call | solution.py:283
  33.8 1.0 collective-permute-start.2
  34.8 0.0 collective-permute-done.other
  34.8 8.5 %shard_map.68 = (f32[384,768]{1,0:T(8,128)S(1)}, f32[384,768]{1,0:T(8,128)S(1)}) custom-call(f32[384,768]{1,0:T(8,128)S(1)} %get-tuple-element.16.mine, f32[384,768]{1,0:T(8,128)S(1)} %collective-permute-done.other, f32[384,768]{1,0:T(8,128)S(1)} %get-tuple-element.20.one, f32[384,768]{1,0:T(8,128)S(1)} %get-tuple-element.21.two, ...), custom_call_target="tpu_custom_call" | custom-call | flops 30000001024 | bytes 1 | tf_op jit(solution)/shard_map/pallas_call | solution.py:283
  43.3 5.2 %collective-permute-start.3 = (f32[384,768]{1,0:T(8,128)S(1)}, f32[384,768]{1,0:T(8,128)S(1)}, u32[]{:S(2)}, u32[]{:S(2)}) collective-permute-start(f32[384,768]{1,0:T(8,128)S(1)} %get-tuple-element.26), channel_id=1, source_target_pairs={{0,16},{32,48},{64,80},{96,112},{1,17},{33,49},{65,81},{97,113},{2... | collective-permute-start | bytes 3538952 | tf_op jit(solution)/shard_map/ppermute | solution.py:307
  48.6 0.0 collective-permute-done.2.border_term
  48.6 0.1 shard_map.69.rest
  48.7 2.2 %collective-permute-done.3.chip_term = f32[384,768]{1,0:T(8,128)S(1)} collective-permute-done((f32[384,768]{1,0:T(8,128)S(1)}, f32[384,768]{1,0:T(8,128)S(1)}, u32[]{:S(2)}, u32[]{:S(2)}) %collective-permute-start.3) | collective-permute-done | bytes 1179680 | tf_op jit(solution)/shard_map/ppermute | solution.py:307
  50.9 4.3 %shard_map.70 = f32[2,384,384]{2,1,0:T(8,128)S(1)} custom-call(f32[384,768]{1,0:T(8,128)S(1)} %shard_map.69.rest, f32[384,768]{1,0:T(8,128)S(1)} %collective-permute-done.3.chip_term), custom_call_target="tpu_custom_call" | custom-call | flops 30000001024 | bytes 1 | tf_op jit(solution)/shard_map/pallas_call | solution.py:283
  55.2 0.0 copy-start
  55.2 0.0 copy-start.1
  55.3 0.0 copy-start.2
  55.3 0.0 copy-start.3
  55.3 26.1 %all_to_all.10 = f32[16,48,384]{2,1,0:T(8,128)S(1)} all-to-all(f32[16,48,384]{2,1,0:T(8,128)S(1)} %bitcast.6), channel_id=1, replica_groups=mesh['layer'=8,'energy'=4,'momentum'=4] {'energy','momentum'}, dimensions={0} | all-to-all | bytes 2359296 | tf_op jit(solution)/shard_map/all_to_all | solution.py:343
  81.4 0.0 copy-done
  81.4 0.0 copy-done.1
  81.4 0.0 copy-done.2
  81.4 0.0 copy-done.3
  81.4 1.6 %shard_map.71 = f32[4,4,48,384]{3,2,1,0:T(8,128)S(1)} custom-call(f32[4,4]{1,0:T(4,128)S(1)} %copy-done, f32[3]{0:T(128)S(1)} %copy-done.1, s32[4]{0:T(128)S(1)} %copy-done.2, s32[3]{0:T(128)S(1)} %copy-done.3, f32[4,4,48,384]{3,2,1,0:T(8,128)S(1)} %bitcast.4), custom_call_target="tpu_custom_call" | custom-call | tf_op jit(solution)/shard_map/pallas_call | solution.py:348
  83.0 21.2 %all_to_all.11 = f32[16,48,384]{2,1,0:T(8,128)S(1)} all-to-all(f32[16,48,384]{2,1,0:T(8,128)S(1)} %bitcast.5), channel_id=1, replica_groups=mesh['layer'=8,'energy'=4,'momentum'=4] {'energy','momentum'}, dimensions={0} | all-to-all | bytes 2359296 | tf_op jit(solution)/shard_map/all_to_all | solution.py:356
  104.2 1.0 copy.8
Async XLA Ops:
  9.9 24.9 %collective-permute-start = (f32[384,768]{1,0:T(8,128)S(1)}, f32[384,768]{1,0:T(8,128)S(1)}, u32[]{:S(2)}, u32[]{:S(2)}) collective-permute-start(f32[384,768]{1,0:T(8,128)S(1)} %get-tuple-element.16.mine), channel_id=1, source_target_pairs={{16,32},{32,16},{48,64},{64,48},{80,96},{96,80},{17,33},{33,17},{4... | collective-permute-start | bytes 3538952 | tf_op jit(solution)/shard_map/ppermute | solution.py:303
  16.7 8.6 %collective-permute-start.1 = (f32[384,768]{1,0:T(8,128)S(1)}, f32[384,768]{1,0:T(8,128)S(1)}, u32[]{:S(2)}, u32[]{:S(2)}) collective-permute-start(f32[384,768]{1,0:T(8,128)S(1)} %get-tuple-element.22.mine), channel_id=1, source_target_pairs={{0,16},{16,0},{32,48},{48,32},{64,80},{80,64},{96,112},{112,96},{1... | collective-permute-start | bytes 3538952 | tf_op jit(solution)/shard_map/ppermute | solution.py:303
  33.8 14.8 %collective-permute-start.2 = (f32[384,768]{1,0:T(8,128)S(1)}, f32[384,768]{1,0:T(8,128)S(1)}, u32[]{:S(2)}, u32[]{:S(2)}) collective-permute-start(f32[384,768]{1,0:T(8,128)S(1)} %get-tuple-element.24.chip_term), channel_id=1, source_target_pairs={{16,32},{48,64},{80,96},{17,33},{49,65},{81,97},{18,34},{50,66},{8... | collective-permute-start | bytes 3538952 | tf_op jit(solution)/shard_map/ppermute | solution.py:307
  43.3 7.6 %collective-permute-start.3 = (f32[384,768]{1,0:T(8,128)S(1)}, f32[384,768]{1,0:T(8,128)S(1)}, u32[]{:S(2)}, u32[]{:S(2)}) collective-permute-start(f32[384,768]{1,0:T(8,128)S(1)} %get-tuple-element.26), channel_id=1, source_target_pairs={{0,16},{32,48},{64,80},{96,112},{1,17},{33,49},{65,81},{97,113},{2... | collective-permute-start | bytes 3538952 | tf_op jit(solution)/shard_map/ppermute | solution.py:307
  55.2 26.2 %copy-start = (f32[4,4]{1,0:T(4,128)S(1)}, f32[4,4]{1,0:T(4,128)}, u32[]{:S(2)}) copy-start(f32[4,4]{1,0:T(4,128)} %phonon.1) | copy-start | bytes 196
  55.2 26.2 %copy-start.1 = (f32[3]{0:T(128)S(1)}, f32[3]{0:T(128)}, u32[]{:S(2)}) copy-start(f32[3]{0:T(128)} %strength.1) | copy-start | bytes 40
  55.3 26.1 %copy-start.2 = (s32[4]{0:T(128)S(1)}, s32[4]{0:T(128)}, u32[]{:S(2)}) copy-start(s32[4]{0:T(128)} %transfer.1) | copy-start | bytes 52
  55.3 26.1 %copy-start.3 = (s32[3]{0:T(128)S(1)}, s32[3]{0:T(128)}, u32[]{:S(2)}) copy-start(s32[3]{0:T(128)} %offset.1) | copy-start | bytes 40
